TPU v7x, 32 devices: a whole 2x2x4 slice. The times are simulated.
32 devices in a mesh: ctx: 8 (over z, x), fsdp: 4 (over y, core).
Axes of the slice: x: 2, y: 2, z: 4, core: 2. Of those that a mesh axis runs over, the one named last changes fastest.
Arguments:
- inputs: bfloat16 [2, 4, 4096, 512], P(None, 'fsdp', 'ctx'), may hold values from -6 to 6
- out_grad: bfloat16 [2, 4, 4096, 512], P(None, 'fsdp', 'ctx'), may hold values from -6 to 6
- segment_ids: int32 [2, 4, 4096], P(None, 'fsdp', 'ctx'), may hold values from 0 to 15, never falling along the last dimension, each value on 1 to 2048 neighbouring positions
- block_order: int32 [16], replicated, may hold values from 0 to 15, each once
- w_qkv: bfloat16 [512, 1536], P('fsdp'), may hold values from -0.25 to 0.25
- w_out: bfloat16 [512, 512], P('fsdp'), may hold values from -1 to 1
- w_up: bfloat16 [512, 2048], P('fsdp'), may hold values from -0.25 to 0.25
- w_down: bfloat16 [2048, 512], P('fsdp'), may hold values from -0.125 to 0.125
- norm1_gain: bfloat16 [512], P('fsdp'), may hold values from 0.25 to 1.75
- norm1_bias: bfloat16 [512], P('fsdp'), may hold values from -2 to 2
- norm2_gain: bfloat16 [512], P('fsdp'), may hold values from 0.25 to 1.75
- norm2_bias: bfloat16 [512], P('fsdp'), may hold values from -2 to 2
- out_bias: bfloat16 [512], P('fsdp'), may hold values from -2 to 2
- up_bias: bfloat16 [2048], P('fsdp'), may hold values from -3 to 3
- down_bias: bfloat16 [512], P('fsdp'), may hold values from -2 to 2
Outputs:
- outputs: bfloat16 [2, 4, 4096, 512], P(None, 'fsdp', 'ctx')
- input_grad: float32 [2, 4, 4096, 512], P(None, 'fsdp', 'ctx')
- grad_w_qkv: float32 [512, 1536], P('fsdp')
- grad_w_out: float32 [512, 512], P('fsdp')
- grad_w_up: float32 [512, 2048], P('fsdp')
- grad_w_down: float32 [2048, 512], P('fsdp')
- grad_norm1_gain: float32 [512], P('fsdp')
- grad_norm1_bias: float32 [512], P('fsdp')
- grad_norm2_gain: float32 [512], P('fsdp')
- grad_norm2_bias: float32 [512], P('fsdp')
- grad_out_bias: float32 [512], P('fsdp')
- grad_up_bias: float32 [2048], P('fsdp')
- grad_down_bias: float32 [512], P('fsdp')
Inputs may be any that keep to these rules, and one draw needn't show every extreme that they name: `segment_ids`: along each sequence's true positions document numbers start at 0 and never fall; each document has 1 to 2048 tokens and one has exactly 2048. `block_order`: each value appears exactly once.
All inputs are finite; a program needn't handle non-finite values.
Results may differ from a plain program's by a relative error of at most 0.02.
Values may be sent and summed in bfloat16 or wider, within the bound.
A program may use at most 256 MiB of HBM per device.

v0:
```python
import math
import jax
import jax.numpy as jnp
from jax import lax
from jax.sharding import PartitionSpec as P

H = 8
HD = 64
BLK = 256
norm_eps = 1e-05
mask_fill = -1e30


def layer_norm(values, gain_vec, offset):
    center = values - jnp.mean(values, axis=-1, keepdims=True)
    spread = jnp.mean(center * center, axis=-1, keepdims=True)
    return center * lax.rsqrt(spread + norm_eps) * gain_vec + offset


def gelu_exact(values):
    return 0.5 * values * (1.0 + lax.erf(values * (1.0 / math.sqrt(2.0))))


def score_block(query_heads, key_heads, query_doc, query_pos, key_doc, key_pos):
    raw_scores = jnp.einsum(
        "qhd,khd->hqk", query_heads, key_heads, preferred_element_type=jnp.float32
    ) * (1.0 / math.sqrt(HD))
    allowed = (query_doc[:, None] == key_doc[None, :]) & (key_pos[None, :] <= query_pos[:, None])
    return (raw_scores, allowed[None])


def soft_block(raw_scores, allowed, log_norm):
    return jnp.exp(jnp.where(allowed, raw_scores, mask_fill) - log_norm[:, :, None])


def row_log_norm(query_heads, key_blocks, doc_blocks, pos_blocks, query_doc, query_pos):

    def row_visit(running, block_item):
        row_top, row_sum = running
        key_heads, key_doc, key_pos = block_item
        raw_scores, allowed = score_block(
            query_heads, key_heads, query_doc, query_pos, key_doc, key_pos
        )
        masked = jnp.where(allowed, raw_scores, mask_fill)
        new_top = jnp.maximum(row_top, jnp.max(masked, axis=-1))
        fresh = jnp.sum(jnp.where(allowed, jnp.exp(masked - new_top[:, :, None]), 0.0), axis=-1)
        return ((new_top, row_sum * jnp.exp(row_top - new_top) + fresh), None)

    query_count = query_doc.shape[0]
    start = (
        jnp.full((H, query_count), mask_fill, jnp.float32),
        jnp.zeros((H, query_count), jnp.float32),
    )
    (row_top, row_sum), unused = lax.scan(row_visit, start, (key_blocks, doc_blocks, pos_blocks))
    return row_top + jnp.log(row_sum)


def attend(
    query_heads, key_blocks, value_blocks, doc_blocks, pos_blocks, query_doc, query_pos, log_norm
):

    def attend_visit(accum_out, block_item):
        key_heads, value_heads, key_doc, key_pos = block_item
        raw_scores, allowed = score_block(
            query_heads, key_heads, query_doc, query_pos, key_doc, key_pos
        )
        soft_low = soft_block(raw_scores, allowed, log_norm).astype(jnp.bfloat16)
        return (
            accum_out
            + jnp.einsum("hqk,khd->qhd", soft_low, value_heads, preferred_element_type=jnp.float32),
            None,
        )

    start = jnp.zeros(query_heads.shape, jnp.float32)
    accum_out, unused = lax.scan(
        attend_visit, start, (key_blocks, value_blocks, doc_blocks, pos_blocks)
    )
    return accum_out


def grad_block(
    query_heads,
    grad_heads,
    log_norm,
    row_delta,
    query_doc,
    query_pos,
    key_heads,
    value_heads,
    key_doc,
    key_pos,
):
    raw_scores, allowed = score_block(
        query_heads, key_heads, query_doc, query_pos, key_doc, key_pos
    )
    soft = soft_block(raw_scores, allowed, log_norm)
    grad_soft = jnp.einsum(
        "qhd,khd->hqk", grad_heads, value_heads, preferred_element_type=jnp.float32
    )
    grad_scores = (soft * (grad_soft - row_delta[:, :, None])).astype(jnp.bfloat16)
    score_scale = 1.0 / math.sqrt(HD)
    part_q = (
        jnp.einsum("hqk,khd->qhd", grad_scores, key_heads, preferred_element_type=jnp.float32)
        * score_scale
    )
    part_k = (
        jnp.einsum("hqk,qhd->khd", grad_scores, query_heads, preferred_element_type=jnp.float32)
        * score_scale
    )
    part_v = jnp.einsum(
        "hqk,qhd->khd", soft.astype(jnp.bfloat16), grad_heads, preferred_element_type=jnp.float32
    )
    return (part_q, part_k, part_v)


def body(
    inputs,
    out_grad,
    segment_ids,
    block_order,
    w_qkv,
    w_out,
    w_up,
    w_down,
    norm1_gain,
    norm1_bias,
    norm2_gain,
    norm2_bias,
    out_bias,
    up_bias,
    down_bias,
):
    gathered = (
        lax.all_gather(w_qkv, "fsdp", axis=0, tiled=True),
        lax.all_gather(w_out, "fsdp", axis=0, tiled=True),
        lax.all_gather(w_up, "fsdp", axis=0, tiled=True),
        lax.all_gather(w_down, "fsdp", axis=0, tiled=True),
        lax.all_gather(norm1_gain, "fsdp", axis=0, tiled=True),
        lax.all_gather(norm1_bias, "fsdp", axis=0, tiled=True),
        lax.all_gather(norm2_gain, "fsdp", axis=0, tiled=True),
        lax.all_gather(norm2_bias, "fsdp", axis=0, tiled=True),
        lax.all_gather(out_bias, "fsdp", axis=0, tiled=True),
        lax.all_gather(up_bias, "fsdp", axis=0, tiled=True),
        lax.all_gather(down_bias, "fsdp", axis=0, tiled=True),
    )
    full_qkv, full_out, full_up, full_down = (gathered[0], gathered[1], gathered[2], gathered[3])
    gain_one, bias_one, gain_two, bias_two, full_obias, full_ubias, full_dbias = [
        member.astype(jnp.float32) for member in gathered[4:]
    ]
    model_width = full_qkv.shape[0]
    local_rows = inputs.shape[2]
    ctx_count = lax.axis_size("ctx")
    seq_len = local_rows * ctx_count
    key_block = min(512, seq_len)
    block_count = seq_len // key_block
    ctx_index = lax.axis_index("ctx")
    row_ids = jnp.arange(local_rows, dtype=jnp.int32)
    own_blocks = lax.dynamic_slice_in_dim(block_order, 2 * ctx_index, 2)
    own_pos = own_blocks[row_ids // BLK] * BLK + row_ids % BLK
    all_ids = jnp.arange(seq_len, dtype=jnp.int32)
    all_pos = block_order[all_ids // BLK] * BLK + all_ids % BLK
    pos_blocks = all_pos.reshape(block_count, key_block)
    grad_sums = [jnp.zeros(member.shape, jnp.float32) for member in gathered]
    outputs_list = []
    input_grads = []
    for micro_idx in range(inputs.shape[0]):
        seq_in = inputs[micro_idx, 0].astype(jnp.float32)
        normed, norm1_pull = jax.vjp(layer_norm, seq_in, gain_one, bias_one)
        normed_low = normed.astype(jnp.bfloat16)
        qkv_out = jnp.dot(normed_low, full_qkv, preferred_element_type=jnp.float32).astype(
            jnp.bfloat16
        )
        query_heads = qkv_out[:, :model_width].reshape(local_rows, H, HD)
        kv_all, doc_all = (
            lax.all_gather(qkv_out[:, model_width:], "ctx", axis=0, tiled=True),
            lax.all_gather(segment_ids[micro_idx, 0], "ctx", axis=0, tiled=True),
        )
        doc_rows = doc_all[all_pos]
        query_doc = doc_all[own_pos]
        kv_heads = kv_all.reshape(block_count, key_block, 2, H, HD)
        key_blocks = kv_heads[:, :, 0]
        value_blocks = kv_heads[:, :, 1]
        doc_blocks = doc_rows.reshape(block_count, key_block)
        log_norm = row_log_norm(query_heads, key_blocks, doc_blocks, pos_blocks, query_doc, own_pos)
        attn_acc = attend(
            query_heads,
            key_blocks,
            value_blocks,
            doc_blocks,
            pos_blocks,
            query_doc,
            own_pos,
            log_norm,
        )
        attn_low = attn_acc.reshape(local_rows, model_width).astype(jnp.bfloat16)
        branch = jnp.dot(attn_low, full_out, preferred_element_type=jnp.float32) + full_obias
        middle = seq_in + branch
        normed_two, norm2_pull = jax.vjp(layer_norm, middle, gain_two, bias_two)
        normed_two_low = normed_two.astype(jnp.bfloat16)
        hidden = jnp.dot(normed_two_low, full_up, preferred_element_type=jnp.float32) + full_ubias
        active, gelu_pull = jax.vjp(gelu_exact, hidden)
        active_low = active.astype(jnp.bfloat16)
        result = middle + (
            jnp.dot(active_low, full_down, preferred_element_type=jnp.float32) + full_dbias
        )
        outputs_list.append(result.astype(jnp.bfloat16))
        grad_y = out_grad[micro_idx, 0]
        grad_y32 = grad_y.astype(jnp.float32)
        grad_sums[3] = grad_sums[3] + jnp.einsum(
            "rf,rd->fd", active_low, grad_y, preferred_element_type=jnp.float32
        )
        grad_sums[10] = grad_sums[10] + jnp.sum(grad_y32, axis=0)
        grad_active = jnp.einsum("rd,fd->rf", grad_y, full_down, preferred_element_type=jnp.float32)
        (grad_hidden,) = gelu_pull(grad_active)
        grad_hidden_low = grad_hidden.astype(jnp.bfloat16)
        grad_sums[2] = grad_sums[2] + jnp.einsum(
            "rd,rf->df", normed_two_low, grad_hidden_low, preferred_element_type=jnp.float32
        )
        grad_sums[9] = grad_sums[9] + jnp.sum(grad_hidden_low.astype(jnp.float32), axis=0)
        grad_normed_two = jnp.einsum(
            "rf,df->rd", grad_hidden_low, full_up, preferred_element_type=jnp.float32
        )
        grad_mid_ln, grad_gain_two, grad_bias_two = norm2_pull(grad_normed_two)
        grad_sums[6] = grad_sums[6] + grad_gain_two
        grad_sums[7] = grad_sums[7] + grad_bias_two
        grad_mid = grad_y32 + grad_mid_ln
        grad_mid_low = grad_mid.astype(jnp.bfloat16)
        grad_sums[1] = grad_sums[1] + jnp.einsum(
            "rd,re->de", attn_low, grad_mid_low, preferred_element_type=jnp.float32
        )
        grad_sums[8] = grad_sums[8] + jnp.sum(grad_mid_low.astype(jnp.float32), axis=0)
        grad_attn_low = jnp.einsum(
            "re,de->rd", grad_mid_low, full_out, preferred_element_type=jnp.float32
        ).astype(jnp.bfloat16)
        grad_heads = grad_attn_low.reshape(local_rows, H, HD)
        row_delta = jnp.sum(grad_heads.astype(jnp.float32) * attn_acc, axis=-1).T

        def back_visit(grad_query, block_item):
            key_heads, value_heads, key_doc, key_pos = block_item
            part_q, part_k, part_v = grad_block(
                query_heads,
                grad_heads,
                log_norm,
                row_delta,
                query_doc,
                own_pos,
                key_heads,
                value_heads,
                key_doc,
                key_pos,
            )
            joined = jnp.concatenate(
                [part_k.reshape(key_block, model_width), part_v.reshape(key_block, model_width)],
                axis=1,
            )
            return (grad_query + part_q, joined)

        grad_query, kv_terms = lax.scan(
            back_visit,
            jnp.zeros((local_rows, H, HD), jnp.float32),
            (key_blocks, value_blocks, doc_blocks, pos_blocks),
        )
        kv_grad = lax.psum_scatter(
            kv_terms.reshape(seq_len, 2 * model_width).astype(jnp.bfloat16),
            "ctx",
            scatter_dimension=0,
            tiled=True,
        ).astype(jnp.float32)
        grad_qkv_low = jnp.concatenate(
            [grad_query.reshape(local_rows, model_width), kv_grad], axis=1
        ).astype(jnp.bfloat16)
        grad_sums[0] = grad_sums[0] + jnp.einsum(
            "rd,re->de", normed_low, grad_qkv_low, preferred_element_type=jnp.float32
        )
        grad_normed = jnp.einsum(
            "re,de->rd", grad_qkv_low, full_qkv, preferred_element_type=jnp.float32
        )
        grad_in_ln, grad_gain_one, grad_bias_one = norm1_pull(grad_normed)
        grad_sums[4] = grad_sums[4] + grad_gain_one
        grad_sums[5] = grad_sums[5] + grad_bias_one
        input_grads.append(grad_mid + grad_in_ln)
    owned = (
        lax.psum_scatter(
            grad_sums[0].astype(jnp.bfloat16), "fsdp", scatter_dimension=0, tiled=True
        ).astype(jnp.float32),
        lax.psum_scatter(
            grad_sums[1].astype(jnp.bfloat16), "fsdp", scatter_dimension=0, tiled=True
        ).astype(jnp.float32),
        lax.psum_scatter(
            grad_sums[2].astype(jnp.bfloat16), "fsdp", scatter_dimension=0, tiled=True
        ).astype(jnp.float32),
        lax.psum_scatter(
            grad_sums[3].astype(jnp.bfloat16), "fsdp", scatter_dimension=0, tiled=True
        ).astype(jnp.float32),
        lax.psum_scatter(
            grad_sums[4].astype(jnp.bfloat16), "fsdp", scatter_dimension=0, tiled=True
        ).astype(jnp.float32),
        lax.psum_scatter(
            grad_sums[5].astype(jnp.bfloat16), "fsdp", scatter_dimension=0, tiled=True
        ).astype(jnp.float32),
        lax.psum_scatter(
            grad_sums[6].astype(jnp.bfloat16), "fsdp", scatter_dimension=0, tiled=True
        ).astype(jnp.float32),
        lax.psum_scatter(
            grad_sums[7].astype(jnp.bfloat16), "fsdp", scatter_dimension=0, tiled=True
        ).astype(jnp.float32),
        lax.psum_scatter(
            grad_sums[8].astype(jnp.bfloat16), "fsdp", scatter_dimension=0, tiled=True
        ).astype(jnp.float32),
        lax.psum_scatter(
            grad_sums[9].astype(jnp.bfloat16), "fsdp", scatter_dimension=0, tiled=True
        ).astype(jnp.float32),
        lax.psum_scatter(
            grad_sums[10].astype(jnp.bfloat16), "fsdp", scatter_dimension=0, tiled=True
        ).astype(jnp.float32),
    )
    summed = (
        lax.psum(owned[0].astype(jnp.bfloat16), "ctx").astype(jnp.float32),
        lax.psum(owned[1].astype(jnp.bfloat16), "ctx").astype(jnp.float32),
        lax.psum(owned[2].astype(jnp.bfloat16), "ctx").astype(jnp.float32),
        lax.psum(owned[3].astype(jnp.bfloat16), "ctx").astype(jnp.float32),
        lax.psum(owned[4].astype(jnp.bfloat16), "ctx").astype(jnp.float32),
        lax.psum(owned[5].astype(jnp.bfloat16), "ctx").astype(jnp.float32),
        lax.psum(owned[6].astype(jnp.bfloat16), "ctx").astype(jnp.float32),
        lax.psum(owned[7].astype(jnp.bfloat16), "ctx").astype(jnp.float32),
        lax.psum(owned[8].astype(jnp.bfloat16), "ctx").astype(jnp.float32),
        lax.psum(owned[9].astype(jnp.bfloat16), "ctx").astype(jnp.float32),
        lax.psum(owned[10].astype(jnp.bfloat16), "ctx").astype(jnp.float32),
    )
    return (
        jnp.stack(outputs_list)[:, None],
        jnp.stack(input_grads)[:, None],
        summed[0],
        summed[1],
        summed[2],
        summed[3],
        summed[4],
        summed[5],
        summed[6],
        summed[7],
        summed[8],
        summed[9],
        summed[10],
    )


def solution(mesh):
    return jax.shard_map(
        body,
        mesh=mesh,
        in_specs=(
            P(None, "fsdp", "ctx", None),
            P(None, "fsdp", "ctx", None),
            P(None, "fsdp", "ctx"),
            P(),
            P("fsdp", None),
            P("fsdp", None),
            P("fsdp", None),
            P("fsdp", None),
            P("fsdp"),
            P("fsdp"),
            P("fsdp"),
            P("fsdp"),
            P("fsdp"),
            P("fsdp"),
            P("fsdp"),
        ),
        out_specs=(
            P(None, "fsdp", "ctx", None),
            P(None, "fsdp", "ctx", None),
            P("fsdp", None),
            P("fsdp", None),
            P("fsdp", None),
            P("fsdp", None),
            P("fsdp"),
            P("fsdp"),
            P("fsdp"),
            P("fsdp"),
            P("fsdp"),
            P("fsdp"),
            P("fsdp"),
        ),
        check_vma=False,
    )
```

profile of v0, /device:TPU:0, one launch (start us, length us, event | category | flops | bytes accessed | tf_op | source)
XLA Modules:
  0.0 1195.3 jit_solution(4293471570105327463)
XLA Ops:
  8.0 6.2 all-gather.2
  14.1 5.4 all-gather.3
  21.4 10.5 all-gather.15.cloned.1.call-done
  45.4 27.0 %all-gather = s32[1,1,4096]{2,1,0:T(1,128)S(1)} all-gather(s32[1,1,512]{2,1,0:T(1,128)S(1)} %get-tuple-element.1148), channel_id=2, replica_groups=mesh['ctx'=8,'fsdp'=4] {'ctx'}, dimensions={2}, use_global_device_ids=true | all-gather | bytes 18432 | tf_op jit(solution)/shard_map/all_gather | solution.py:176
  76.7 5.7 select_multiply_fusion.2
  85.7 23.0 %gather_fusion.1 = s32[4096]{0:T(1024)S(1)} fusion(s32[4096]{0:T(1024)S(1)} %bitcast.527, s32[4096]{0:T(1024)S(1)} %broadcast_clamp_fusion), kind=kCustom, calls=%fused_computation.1 | custom fusion | bytes 49152 | tf_op jit(solution)/shard_map/gather | solution.py:178
  108.7 26.7 %all-gather.1 = s32[1,1,4096]{2,1,0:T(1,128)S(1)} all-gather(s32[1,1,512]{2,1,0:T(1,128)S(1)} %get-tuple-element.1149), channel_id=3, replica_groups=mesh['ctx'=8,'fsdp'=4] {'ctx'}, dimensions={2}, use_global_device_ids=true | all-gather | bytes 18432 | tf_op jit(solution)/shard_map/all_gather | solution.py:176
  138.6 23.0 %gather_fusion.3 = s32[4096]{0:T(1024)S(1)} fusion(s32[4096]{0:T(1024)S(1)} %bitcast.529, s32[4096]{0:T(1024)S(1)} %broadcast_clamp_fusion), kind=kCustom, calls=%fused_computation.3 | custom fusion | bytes 49152 | tf_op jit(solution)/shard_map/gather | solution.py:178
  182.3 7.2 all_gather.50
  195.1 11.4 copy.162
  206.6 12.2 %copy.239 = bf16[128,8,8,512]{3,2,1,0:T(8,128)(2,1)} copy(bf16[128,8,8,512]{3,1,2,0:T(8,128)(2,1)} %bitcast.538) | data formatting | bytes 16777216
  218.8 5.3 slice_bitcast_fusion
  227.5 50.1 %while.76 = (s32[]{:T(128)}, f32[8,512]{1,0:T(8,128)S(1)}, f32[8,512]{1,0:T(8,128)S(1)}, s32[512]{0:T(512)S(1)}, s32[8,512]{1,0:T(8,128)S(1)}, /*index=5*/s32[8,...) while((s32[]{:T(128)}, f32[8,512]{1,0:T(8,128)S(1)}, ...), condition=%wide.region_15.16_spmd.clone, body=%wide.region_12.15_spmd.clone.sunk | while | flops 286030336 | bytes 18847896 | solution.py:54
  277.6 10.2 all-gather.17.cloned.1.call-done
  287.8 11.7 copy.155
  299.6 12.2 %copy.238 = bf16[128,8,8,512]{3,2,1,0:T(8,128)(2,1)} copy(bf16[128,8,8,512]{3,1,2,0:T(8,128)(2,1)} %bitcast.539) | data formatting | bytes 16777216
  320.5 50.5 %while.74 = (s32[]{:T(128)}, f32[8,512]{1,0:T(8,128)S(1)}, f32[8,512]{1,0:T(8,128)S(1)}, s32[512]{0:T(512)S(1)}, s32[8,512]{1,0:T(8,128)S(1)}, /*index=5*/s32[8,...) while((s32[]{:T(128)}, f32[8,512]{1,0:T(8,128)S(1)}, ...), condition=%wide.region_5.6_spmd.clone, body=%wide.region_2.5_spmd.clone.sunk | while | flops 286030336 | bytes 18847896 | solution.py:54
  371.0 5.7 copy.158
  377.3 46.4 %while.75 = (s32[]{:T(128)}, f32[512,8,64]{0,2,1:T(8,128)S(1)}, bf16[8,512,8,64]{1,3,2,0:T(8,128)(2,1)}, s32[512]{0:T(512)S(1)}, s32[8,512]{1,0:T(8,128)S(1)}, /...) while((s32[]{:T(128)}, f32[512,8,64]{0,2,1:T(8,128)S(1)}, ...), condition=%wide.region_7.8_spmd.clone, body=%wide.region_6.7_spmd.clone.sunk | while | flops 546580992 | bytes 4234906 | solution.py:75
  424.7 5.7 copy.165
  430.4 46.4 %while.77 = (s32[]{:T(128)}, f32[512,8,64]{0,2,1:T(8,128)S(1)}, bf16[8,512,8,64]{1,3,2,0:T(8,128)(2,1)}, s32[512]{0:T(512)S(1)}, s32[8,512]{1,0:T(8,128)S(1)}, /...) while((s32[]{:T(128)}, f32[512,8,64]{0,2,1:T(8,128)S(1)}, ...), condition=%wide.region_17.18_spmd.clone, body=%wide.region_16.17_spmd.clone.sunk | while | flops 546580992 | bytes 4234906 | solution.py:75
  486.4 5.9 convert_reduce_fusion
  497.7 6.1 multiply_convert_fusion.1
  525.5 138.9 %while.78 = (s32[]{:T(128)}, f32[512,8,64]{0,2,1:T(8,128)}, bf16[8,512,1024]{2,1,0:T(8,128)(2,1)}, bf16[8,512,8,64]{1,3,2,0:T(8,128)(2,1)}, s32[512]{0:T(512)S(1...) while((s32[]{:T(128)}, f32[512,8,64]{0,2,1:T(8,128)}, ...), condition=%wide.region_24.25_spmd.clone, body=%wide.region_23.24_spmd.clone.sunk | while | flops 1367353856 | bytes 51714240 | solution.py:258
  668.7 131.5 %while.79 = (s32[]{:T(128)}, f32[512,8,64]{0,2,1:T(8,128)}, bf16[8,512,1024]{2,1,0:T(8,128)(2,1)}, bf16[8,512,8,64]{1,3,2,0:T(8,128)(2,1)}, s32[512]{0:T(512)S(1...) while((s32[]{:T(128)}, f32[512,8,64]{0,2,1:T(8,128)}, ...), condition=%wide.region_32.33_spmd.clone, body=%wide.region_31.32_spmd.clone.sunk | while | flops 1367353856 | bytes 51714240 | solution.py:258
  834.8 129.0 %reduce-scatter.9.cloned.1.call-done = bf16[512,1024]{1,0:T(8,128)(2,1)} async-done(((bf16[4096,1024]{1,0:T(8,128)(2,1)}), bf16[512,1024]{1,0:T(8,128)(2,1)}) %reduce-scatter.9.cloned.1.call-update) | async-done | bytes 1048592 | tf_op jit(solution)/shard_map/reduce_scatter | solution.py:263
  987.0 34.2 %reduce-scatter.15.cloned.1.call-done = bf16[128,2048]{1,0:T(8,128)(2,1)} async-done(((bf16[512,2048]{1,0:T(8,128)(2,1)}), bf16[128,2048]{1,0:T(8,128)(2,1)}) %reduce-scatter.15.cloned.1.call-update) | async-done | bytes 524304 | tf_op jit(solution)/shard_map/reduce_scatter | solution.py:289
  1021.1 33.9 %reduce-scatter.17.cloned.1.call-done = bf16[512,512]{1,0:T(8,128)(2,1)} async-done(((bf16[2048,512]{1,0:T(8,128)(2,1)}), bf16[512,512]{1,0:T(8,128)(2,1)}) %reduce-scatter.17.cloned.1.call-update) | async-done | bytes 524304 | tf_op jit(solution)/shard_map/reduce_scatter | solution.py:292
  1055.0 31.5 %reduce-scatter.11.cloned.1.call-done = bf16[128,1536]{1,0:T(8,128)(2,1)} async-done(((bf16[512,1536]{1,0:T(8,128)(2,1)}), bf16[128,1536]{1,0:T(8,128)(2,1)}) %reduce-scatter.11.cloned.1.call-update) | async-done | bytes 393232 | tf_op jit(solution)/shard_map/reduce_scatter | solution.py:283
  1091.7 10.5 all-reduce.9
  1102.8 22.1 %all-reduce.7 = (bf16[128]{0:T(256)(128)(2,1)S(1)}, bf16[128]{0:T(256)(128)(2,1)S(1)}, bf16[128]{0:T(256)(128)(2,1)S(1)}, bf16[128]{0:T(256)(128)(2,1)S(1)}, bf1...) all-reduce(bf16[128]{0:T(256)(128)(2,1)S(1)} %dynamic-slice.1, ...), channel_id=1, replica_groups=mesh['ctx'=8,'fsdp'=4] {'ctx'}, use_global_device_ids=true, to_apply=%region_47.48 | all-reduce | flops 1280 | bytes 5120 | tf_op jit(solution)/shard_map/psum | solution.py:322
  1131.7 48.7 %all-reduce.12.cloned.1.call-done = (bf16[128,1536]{1,0:T(8,128)(2,1)}, bf16[128,512]{1,0:T(8,128)(2,1)}, bf16[128,2048]{1,0:T(8,128)(2,1)}, bf16[512,512]{1,0:T(8,128)(2,1)}) async-done(((bf16[128,1536]{1,0:T(8,128)(2,1)}, bf16[128,512]{1,0:T(8,128)(2,1)}, bf16[128,2048]{1,0:T(8,128)(2,1)}, bf16[512,512]{1,0:T(8,128)(2,1)}), (bf16[128,1536]{1,0:T(8,128)(2,1)}, bf16[128,512]{1,0:T(8,128)(2,1)}, ...) | async-done | bytes 1572880 | tf_op jit(solution)/shard_map/psum | solution.py:318
  (799 shorter events, 643.1 us)
Async XLA Ops:
  7.2 24.8 %all-gather.15.cloned.1.call-start = ((), (), s32[]{:S(2)}) async-start(), calls=%async_computation.6 | async-start | bytes 1966080 | tf_op jit(solution)/shard_map/all_gather | solution.py:134
  7.9 187.2 %all-gather.23.cloned.1.call-start = ((), (), s32[]{:S(2)}) async-start(), calls=%async_computation.10 | async-start | bytes 9437184 | tf_op jit(solution)/shard_map/all_gather | solution.py:175
  36.8 251.0 %all-gather.17.cloned.1.call-start = ((), (), s32[]{:S(2)}) async-start(), calls=%async_computation.7 | async-start | bytes 9437184 | tf_op jit(solution)/shard_map/all_gather | solution.py:175
  37.1 441.5 %copy-start.7 = (bf16[1,1,512,512]{2,3,1,0:T(8,128)(2,1)}, bf16[1,1,512,512]{2,3,1,0:T(8,128)(2,1)S(1)}, u32[]{:S(2)}) copy-start(bf16[1,1,512,512]{2,3,1,0:T(8,128)(2,1)S(1)} %copy.202) | copy-start | bytes 1572868
  40.9 440.4 %all-gather.19.cloned.1.call-start = ((), (), s32[]{:S(2)}) async-start(), calls=%async_computation.8 | async-start | bytes 2621440 | tf_op jit(solution)/shard_map/all_gather | solution.py:136
  41.5 444.9 %all-gather.21.cloned.1.call-start = ((), (), s32[]{:S(2)}) async-start(), calls=%async_computation.9 | async-start | bytes 2621440 | tf_op jit(solution)/shard_map/all_gather | solution.py:137
  42.1 788.4 %reduce-scatter.7.cloned.1.call-start = ((), (), s32[]{:S(2)}) async-start(), calls=%async_computation.11 | async-start | bytes 9437184 | tf_op jit(solution)/shard_map/reduce_scatter | solution.py:263
  138.6 38.4 %copy-start.91 = (bf16[512]{0:T(512)(128)(2,1)S(1)}, bf16[512]{0:T(512)(128)(2,1)}, u32[]{:S(2)}) copy-start(bf16[512]{0:T(512)(128)(2,1)} %param.40) | copy-start | bytes 3076
  138.6 43.7 %copy-start.51 = (bf16[128,512]{1,0:T(8,128)(2,1)S(1)}, bf16[128,512]{1,0:T(8,128)(2,1)}, u32[]{:S(2)}) copy-start(bf16[128,512]{1,0:T(8,128)(2,1)} %param.32) | copy-start | bytes 393220
  138.6 50.9 %copy-start.28 = (bf16[2,1,512,512]{3,2,1,0:T(8,128)(2,1)S(1)}, bf16[2,1,512,512]{3,2,1,0:T(8,128)(2,1)}, u32[]{:S(2)}) copy-start(bf16[2,1,512,512]{3,2,1,0:T(8,128)(2,1)} %param.28) | copy-start | bytes 3145732
  167.0 349.0 %copy-start.47 = (f32[4,1,128]{2,1,0:T(1,128)}, f32[4,1,128]{2,1,0:T(1,128)S(1)}, u32[]{:S(2)}) copy-start(f32[4,1,128]{2,1,0:T(1,128)S(1)} %convert_element_type.307) | copy-start | bytes 6148
  172.0 325.7 %copy-start.53 = (f32[4,1,128]{2,1,0:T(1,128)}, f32[4,1,128]{2,1,0:T(1,128)S(1)}, u32[]{:S(2)}) copy-start(f32[4,1,128]{2,1,0:T(1,128)S(1)} %convert_element_type.308) | copy-start | bytes 6148
  189.5 289.0 %copy-start.9 = (bf16[512,512]{1,0:T(8,128)(2,1)}, bf16[512,512]{1,0:T(8,128)(2,1)S(1)}, u32[]{:S(2)}) copy-start(bf16[512,512]{1,0:T(8,128)(2,1)S(1)} %all_gather.50) | copy-start | bytes 1572868
  479.1 36.9 %copy-start.2 = (f32[512,512]{0,1:T(8,128)}, f32[512,512]{0,1:T(8,128)S(1)}, u32[]{:S(2)}) copy-start(f32[512,512]{0,1:T(8,128)S(1)} %get-tuple-element.1175) | copy-start | bytes 3145732
  479.1 36.9 %copy-start.57 = (f32[512]{0:T(512)}, f32[512]{0:T(512)S(1)}, u32[]{:S(2)}) copy-start(f32[512]{0:T(512)S(1)} %broadcast_multiply_fusion.2) | copy-start | bytes 6148
  481.0 35.0 %copy-start = (f32[512,512]{0,1:T(8,128)}, f32[512,512]{0,1:T(8,128)S(1)}, u32[]{:S(2)}) copy-start(f32[512,512]{0,1:T(8,128)S(1)} %get-tuple-element.1177) | copy-start | bytes 3145732
  481.1 35.0 %copy-start.49 = (f32[512]{0:T(512)}, f32[512]{0:T(512)S(1)}, u32[]{:S(2)}) copy-start(f32[512]{0:T(512)S(1)} %broadcast_multiply_fusion) | copy-start | bytes 6148
  481.3 34.8 %copy-start.55 = (f32[512]{0:T(512)}, f32[512]{0:T(512)S(1)}, u32[]{:S(2)}) copy-start(f32[512]{0:T(512)S(1)} %get-tuple-element.1196) | copy-start | bytes 6148
  481.3 34.8 %copy-start.65 = (f32[512]{0:T(512)}, f32[512]{0:T(512)S(1)}, u32[]{:S(2)}) copy-start(f32[512]{0:T(512)S(1)} %get-tuple-element.1195) | copy-start | bytes 6148
  664.4 299.4 %reduce-scatter.9.cloned.1.call-start = ((), (), s32[]{:S(2)}) async-start(), calls=%async_computation.12 | async-start | bytes 9437184 | tf_op jit(solution)/shard_map/reduce_scatter | solution.py:263
  800.3 186.7 %reduce-scatter.13.cloned.1.call-start = ((), (), s32[]{:S(2)}) async-start(), calls=%async_computation.14 | async-start | bytes 655360 | tf_op jit(solution)/shard_map/reduce_scatter | solution.py:286
  803.2 218.0 %reduce-scatter.15.cloned.1.call-start = ((), (), s32[]{:S(2)}) async-start(), calls=%async_computation.15 | async-start | bytes 2621440 | tf_op jit(solution)/shard_map/reduce_scatter | solution.py:289
  809.2 245.8 %reduce-scatter.17.cloned.1.call-start = ((), (), s32[]{:S(2)}) async-start(), calls=%async_computation.16 | async-start | bytes 2621440 | tf_op jit(solution)/shard_map/reduce_scatter | solution.py:292
  815.1 271.4 %reduce-scatter.11.cloned.1.call-start = ((), (), s32[]{:S(2)}) async-start(), calls=%async_computation.13 | async-start | bytes 1966080 | tf_op jit(solution)/shard_map/reduce_scatter | solution.py:283
  830.5 133.3 %copy-start.6 = (bf16[1,1,512,512]{2,3,1,0:T(8,128)(2,1)S(1)}, bf16[1,1,512,512]{2,3,1,0:T(8,128)(2,1)}, u32[]{:S(2)}) copy-start(bf16[1,1,512,512]{2,3,1,0:T(8,128)(2,1)} %copy-done.4) | copy-start | bytes 1572868
  830.5 133.3 %copy-start.62 = (f32[512]{0:T(512)S(1)}, f32[512]{0:T(512)}, u32[]{:S(2)}) copy-start(f32[512]{0:T(512)} %copy-done.61) | copy-start | bytes 6148
  830.5 133.3 %copy-start.68 = (f32[512]{0:T(512)S(1)}, f32[512]{0:T(512)}, u32[]{:S(2)}) copy-start(f32[512]{0:T(512)} %copy-done.67) | copy-start | bytes 6148
  968.2 212.2 %all-reduce.12.cloned.1.call-start = ((), (), s32[]{:S(2)}) async-start(), calls=%async_computation.17 | async-start | bytes 3145728 | tf_op jit(solution)/shard_map/psum | solution.py:318
  981.3 105.2 %copy-start.27 = (bf16[1,1,512,512]{2,3,1,0:T(8,128)(2,1)S(1)}, bf16[1,1,512,512]{2,3,1,0:T(8,128)(2,1)}, u32[]{:S(2)}) copy-start(bf16[1,1,512,512]{2,3,1,0:T(8,128)(2,1)} %copy.204) | copy-start | bytes 1572868
  981.3 105.2 %copy-start.78 = (f32[512]{0:T(512)S(1)}, f32[512]{0:T(512)}, u32[]{:S(2)}) copy-start(f32[512]{0:T(512)} %copy-done.77) | copy-start | bytes 6148
  986.3 103.6 %copy-start.23 = (bf16[1,1,512,512]{2,3,1,0:T(8,128)(2,1)S(1)}, bf16[1,1,512,512]{2,3,1,0:T(8,128)(2,1)}, u32[]{:S(2)}) copy-start(bf16[1,1,512,512]{2,3,1,0:T(8,128)(2,1)} %copy.205) | copy-start | bytes 1572868
  986.3 103.6 %copy-start.76 = (f32[512]{0:T(512)S(1)}, f32[512]{0:T(512)}, u32[]{:S(2)}) copy-start(f32[512]{0:T(512)} %copy-done.75) | copy-start | bytes 6148
  (80 other events, 435.9 us)
Sparse Core Ops, SparseCore 0:
  9.6 22.3 all-gather.14
  36.9 125.5 all-gather.22
  164.7 123.0 all-gather.16
  289.2 20.7 all-gather.18
  311.5 22.5 all-gather.20
  664.5 147.1 reduce-scatter.6
  815.8 147.9 reduce-scatter.8
  966.3 20.6 reduce-scatter.12
  989.7 31.4 reduce-scatter.14
  1023.5 31.4 reduce-scatter.16
  1058.3 28.1 reduce-scatter.10
  1090.2 90.2 all-reduce.11
where the time goes:
time: 1210 us; the launch traced here: 1200 us
  matrix products  395 us (33%)
  waiting for transfers between devices  301 us (25%)
  local copies, waits for them, and re-layouts  193 us (16%)
  other arithmetic  155 us (13%)
  blocking collectives  131 us (11%)
  between operations  17.2 us (1%)
    reduce_scatter x2, waiting for transfers between devices, body(): lax.psum_scatter(kv_terms.reshape(seq_len, 2 * model_width).astype(jnp.bf...  129 us
    dot_general x32, matrix products, score_block(): jnp.einsum('qhd,khd->hqk', query_heads, key_heads, preferred_element_type...  77.9 us
    dot_general x16, matrix products, attend_visit(): jnp.einsum('hqk,khd->qhd', soft_low, value_heads, preferred_element_type=...  66.4 us
    dot_general x16, matrix products, grad_block(): jnp.einsum('qhd,khd->hqk', grad_heads, value_heads, preferred_element_typ...  64.5 us
    mul x48, other arithmetic, body(): own_pos = own_blocks[row_ids // BLK] * BLK + row_ids % BLK  62.6 us
    unnamed x219, local copies, waits for them, and re-layouts  55.3 us
    all_gather x2, blocking collectives, body(): lax.all_gather(segment_ids[micro_idx, 0], 'ctx', axis=0, tiled=True)  53.6 us
    dot_general x16, matrix products, grad_block(): jnp.einsum('hqk,khd->qhd', grad_scores, key_heads, preferred_element_type...  50 us
  transfers between devices with their start and end apart: 12, of which 8 were waited for; matrix products, arithmetic and copies ran while one was open for 46% of the time, Pallas kernels for 0%

commit v1 on v0

--- a/solution.py
+++ b/solution.py
@@ -9,6 +9,18 @@
 BLK = 256
 norm_eps = 1e-05
 mask_fill = -1e30
+
+
+def gather_around(value, axis, dim):
+    ways, here, step = (lax.axis_size(axis), lax.axis_index(axis), value.shape[dim])
+    shape = [n * ways if d == dim else n for d, n in enumerate(value.shape)]
+    full = lax.dynamic_update_slice_in_dim(
+        jnp.zeros(shape, value.dtype), value, here * step, axis=dim
+    )
+    for far in range(1, ways):
+        value = lax.ppermute(value, axis, [(d, (d + 1) % ways) for d in range(ways)])
+        full = lax.dynamic_update_slice_in_dim(full, value, (here - far) % ways * step, axis=dim)
+    return full
 
 
 def layer_norm(values, gain_vec, offset):
@@ -172,7 +184,7 @@
         )
         query_heads = qkv_out[:, :model_width].reshape(local_rows, H, HD)
         kv_all, doc_all = (
-            lax.all_gather(qkv_out[:, model_width:], "ctx", axis=0, tiled=True),
+            gather_around(qkv_out[:, model_width:], "ctx", 0),
             lax.all_gather(segment_ids[micro_idx, 0], "ctx", axis=0, tiled=True),
         )
         doc_rows = doc_all[all_pos]

time: 1210 us -> 1700 us (1.40)
  matrix products: 395 us -> 582 us
  waiting for transfers between devices: 301 us -> 477 us
  other arithmetic: 155 us -> 195 us
  local copies, waits for them, and re-layouts: 193 us -> 229 us
  blocking collectives: 131 us -> 166 us
    ppermute x0 -> x14, waiting for transfers between devices: none -> 206 us  [gather_around(): lax.ppermute(value, axis, [(d, (d + 1) % ways) for d in range(ways)])]
    dot_general x32, matrix products: 77.9 us -> 130 us  [score_block(): jnp.einsum('qhd,khd->hqk', query_heads, key_heads, preferred_element_type...]
    dot_general x16, matrix products: 42.6 us -> 91.9 us  [grad_block(): jnp.einsum('hqk,qhd->khd', soft.astype(jnp.bfloat16), grad_heads, preferr...]
    dot_general x16, matrix products: 64.5 us -> 110 us  [grad_block(): jnp.einsum('qhd,khd->hqk', grad_heads, value_heads, preferred_element_typ...]
    reduce_sum x16, other arithmetic: 32.5 us -> 71.7 us  [row_visit(): jnp.sum(jnp.where(allowed, jnp.exp(masked - new_top[:, :, None]), 0.0), a...]
    all_gather x2, blocking collectives: 53.6 us -> 89.1 us  [body(): lax.all_gather(segment_ids[micro_idx, 0], 'ctx', axis=0, tiled=True)]
    ppermute x0 -> x14, local copies, waits for them, and re-layouts: none -> 26.4 us  [gather_around(): lax.ppermute(value, axis, [(d, (d + 1) % ways) for d in range(ways)])]
    dynamic_update_slice x0 -> x15, local copies, waits for them, and re-layouts: none -> 24.9 us  [the longest x13 23.7 us: gather_around(): lax.dynamic_update_slice_in_dim(full, value, (here - far) % ways * step,...]
  transfers between devices with their start and end apart: 12 -> 24, of which waited for: 8 -> 16; matrix products, arithmetic and copies ran while one was open for 46% -> 45% of each run, Pallas kernels for 0% -> 0%
where the time goes in v1:
time: 1700 us; the launch traced here: 1680 us
  matrix products  582 us (34%)
  waiting for transfers between devices  477 us (28%)
  local copies, waits for them, and re-layouts  229 us (13%)
  other arithmetic  195 us (11%)
  blocking collectives  166 us (10%)
  between operations  17.8 us (1%)
    ppermute x14, waiting for transfers between devices, gather_around(): lax.ppermute(value, axis, [(d, (d + 1) % ways) for d in range(ways)])  206 us
    dot_general x32, matrix products, score_block(): jnp.einsum('qhd,khd->hqk', query_heads, key_heads, preferred_element_type...  130 us
    reduce_scatter x2, waiting for transfers between devices, body(): lax.psum_scatter(kv_terms.reshape(seq_len, 2 * model_width).astype(jnp.bf...  111 us
    dot_general x16, matrix products, grad_block(): jnp.einsum('qhd,khd->hqk', grad_heads, value_heads, preferred_element_typ...  110 us
    dot_general x16, matrix products, grad_block(): jnp.einsum('hqk,qhd->khd', soft.astype(jnp.bfloat16), grad_heads, preferr...  91.9 us
    all_gather x2, blocking collectives, body(): lax.all_gather(segment_ids[micro_idx, 0], 'ctx', axis=0, tiled=True)  89.1 us
    dot_general x16, matrix products, attend_visit(): jnp.einsum('hqk,khd->qhd', soft_low, value_heads, preferred_element_type=...  84.7 us
    reduce_sum x16, other arithmetic, row_visit(): jnp.sum(jnp.where(allowed, jnp.exp(masked - new_top[:, :, None]), 0.0), a...  71.7 us
  transfers between devices with their start and end apart: 24, of which 16 were waited for; matrix products, arithmetic and copies ran while one was open for 45% of the time, Pallas kernels for 0%

profile of v1, /device:TPU:0, one launch (start us, length us, event | category | flops | bytes accessed | tf_op | source)
XLA Modules:
  0.0 1683.2 jit_solution(3089020364499762147)
XLA Ops:
  23.0 9.0 all-gather.13.cloned.1.call-done
  39.3 24.3 %collective-permute-done.7 = bf16[512,1024]{1,0:T(8,128)(2,1)S(1)} collective-permute-done((bf16[512,1024]{1,0:T(8,128)(2,1)S(1)}, bf16[512,1024]{1,0:T(8,128)(2,1)S(1)}, u32[]{:S(2)}, u32[]{:S(2)}) %collective-permute-start.7) | collective-permute-done | bytes 1048608 | tf_op jit(solution)/shard_map/ppermute | solution.py:21
  63.6 22.5 %collective-permute-done = bf16[512,1024]{1,0:T(8,128)(2,1)S(1)} collective-permute-done((bf16[512,1024]{1,0:T(8,128)(2,1)S(1)}, bf16[512,1024]{1,0:T(8,128)(2,1)S(1)}, u32[]{:S(2)}, u32[]{:S(2)}) %collective-permute-start) | collective-permute-done | bytes 1048608 | tf_op jit(solution)/shard_map/ppermute | solution.py:21
  86.1 22.4 %collective-permute-done.8 = bf16[512,1024]{1,0:T(8,128)(2,1)S(1)} collective-permute-done((bf16[512,1024]{1,0:T(8,128)(2,1)S(1)}, bf16[512,1024]{1,0:T(8,128)(2,1)S(1)}, u32[]{:S(2)}, u32[]{:S(2)}) %collective-permute-start.8) | collective-permute-done | bytes 1048608 | tf_op jit(solution)/shard_map/ppermute | solution.py:21
  108.6 22.5 %collective-permute-done.1 = bf16[512,1024]{1,0:T(8,128)(2,1)S(1)} collective-permute-done((bf16[512,1024]{1,0:T(8,128)(2,1)S(1)}, bf16[512,1024]{1,0:T(8,128)(2,1)S(1)}, u32[]{:S(2)}, u32[]{:S(2)}) %collective-permute-start.1) | collective-permute-done | bytes 1048608 | tf_op jit(solution)/shard_map/ppermute | solution.py:21
  136.9 16.6 collective-permute-done.9
  153.5 22.6 %collective-permute-done.2 = bf16[512,1024]{1,0:T(8,128)(2,1)} collective-permute-done((bf16[512,1024]{1,0:T(8,128)(2,1)S(1)}, bf16[512,1024]{1,0:T(8,128)(2,1)}, u32[]{:S(2)}, u32[]{:S(2)}) %collective-permute-start.2) | collective-permute-done | bytes 1048608 | tf_op jit(solution)/shard_map/ppermute | solution.py:21
  182.0 16.6 collective-permute-done.10
  198.6 22.5 %collective-permute-done.3 = bf16[512,1024]{1,0:T(8,128)(2,1)} collective-permute-done((bf16[512,1024]{1,0:T(8,128)(2,1)}, bf16[512,1024]{1,0:T(8,128)(2,1)}, u32[]{:S(2)}, u32[]{:S(2)}) %collective-permute-start.3) | collective-permute-done | bytes 1048608 | tf_op jit(solution)/shard_map/ppermute | solution.py:21
  221.3 63.1 %all-gather.1 = s32[1,1,4096]{2,1,0:T(1,128)S(1)} all-gather(s32[1,1,512]{2,1,0:T(1,128)S(1)} %get-tuple-element.1149), channel_id=3, replica_groups=mesh['ctx'=8,'fsdp'=4] {'ctx'}, dimensions={2}, use_global_device_ids=true | all-gather | bytes 18432 | tf_op jit(solution)/shard_map/all_gather | solution.py:188
  289.5 23.0 %gather_fusion.3 = s32[4096]{0:T(1024)S(1)} fusion(s32[4096]{0:T(1024)S(1)} %bitcast.527, s32[4096]{0:T(1024)S(1)} %broadcast_clamp_fusion), kind=kCustom, calls=%fused_computation.3 | custom fusion | bytes 49152 | tf_op jit(solution)/shard_map/gather | solution.py:190
  312.5 26.0 %all-gather = s32[1,1,4096]{2,1,0:T(1,128)S(1)} all-gather(s32[1,1,512]{2,1,0:T(1,128)S(1)} %get-tuple-element.1148), channel_id=2, replica_groups=mesh['ctx'=8,'fsdp'=4] {'ctx'}, dimensions={2}, use_global_device_ids=true | all-gather | bytes 18432 | tf_op jit(solution)/shard_map/all_gather | solution.py:188
  341.7 23.0 %gather_fusion.1 = s32[4096]{0:T(1024)S(1)} fusion(s32[4096]{0:T(1024)S(1)} %bitcast.529, s32[4096]{0:T(1024)S(1)} %broadcast_clamp_fusion), kind=kCustom, calls=%fused_computation.1 | custom fusion | bytes 49152 | tf_op jit(solution)/shard_map/gather | solution.py:190
  387.9 7.4 all_gather.43
  428.2 18.6 %collective-permute-done.5 = bf16[512,1024]{1,0:T(8,128)(2,1)} collective-permute-done((bf16[512,1024]{1,0:T(8,128)(2,1)}, bf16[512,1024]{1,0:T(8,128)(2,1)}, u32[]{:S(2)}, u32[]{:S(2)}) %collective-permute-start.5) | collective-permute-done | bytes 1048608 | tf_op jit(solution)/shard_map/ppermute | solution.py:21
  473.6 17.6 %collective-permute-done.6 = bf16[512,1024]{1,0:T(8,128)(2,1)} collective-permute-done((bf16[512,1024]{1,0:T(8,128)(2,1)}, bf16[512,1024]{1,0:T(8,128)(2,1)}, u32[]{:S(2)}, u32[]{:S(2)}) %collective-permute-start.6) | collective-permute-done | bytes 1048608 | tf_op jit(solution)/shard_map/ppermute | solution.py:21
  496.1 12.3 copy.277
  519.3 104.3 %while.76 = (s32[]{:T(128)}, f32[8,512]{1,0:T(8,128)S(1)}, f32[8,512]{1,0:T(8,128)S(1)}, s32[512]{0:T(512)S(1)}, s32[8,512]{1,0:T(8,128)S(1)}, /*index=5*/s32[8,...) while((s32[]{:T(128)}, f32[8,512]{1,0:T(8,128)S(1)}, ...), condition=%wide.region_15.16_spmd.clone, body=%wide.region_12.15_spmd.clone.sunk | while | flops 286030336 | bytes 18847896 | solution.py:66
  623.6 55.4 %while.77 = (s32[]{:T(128)}, f32[512,8,64]{0,2,1:T(8,128)}, bf16[8,512,8,64]{1,3,2,0:T(8,128)(2,1)}, s32[512]{0:T(512)S(1)}, s32[8,512]{1,0:T(8,128)S(1)}, /*ind...) while((s32[]{:T(128)}, f32[512,8,64]{0,2,1:T(8,128)}, ...), condition=%wide.region_17.18_spmd.clone, body=%wide.region_16.17_spmd.clone.sunk | while | flops 546580992 | bytes 4234906 | solution.py:87
  679.0 12.5 copy.276
  702.6 95.8 %while.74 = (s32[]{:T(128)}, f32[8,512]{1,0:T(8,128)S(1)}, f32[8,512]{1,0:T(8,128)S(1)}, s32[512]{0:T(512)S(1)}, s32[8,512]{1,0:T(8,128)S(1)}, /*index=5*/s32[8,...) while((s32[]{:T(128)}, f32[8,512]{1,0:T(8,128)S(1)}, ...), condition=%wide.region_5.6_spmd.clone, body=%wide.region_2.5_spmd.clone.sunk | while | flops 286030336 | bytes 18847896 | solution.py:66
  798.5 55.4 %while.75 = (s32[]{:T(128)}, f32[512,8,64]{0,2,1:T(8,128)}, bf16[8,512,8,64]{1,3,2,0:T(8,128)(2,1)}, s32[512]{0:T(512)S(1)}, s32[8,512]{1,0:T(8,128)S(1)}, /*ind...) while((s32[]{:T(128)}, f32[512,8,64]{0,2,1:T(8,128)}, ...), condition=%wide.region_7.8_spmd.clone, body=%wide.region_6.7_spmd.clone.sunk | while | flops 546580992 | bytes 4234906 | solution.py:87
  904.7 194.4 %while.78 = (s32[]{:T(128)}, f32[512,8,64]{0,2,1:T(8,128)}, bf16[8,512,1024]{2,1,0:T(8,128)(2,1)}, bf16[8,512,8,64]{1,3,2,0:T(8,128)(2,1)}, s32[512]{0:T(512)S(1...) while((s32[]{:T(128)}, f32[512,8,64]{0,2,1:T(8,128)}, ...), condition=%wide.region_24.25_spmd.clone, body=%wide.region_23.24_spmd.clone.sunk | while | flops 1367353856 | bytes 102045944 | solution.py:270
  1005.9 7.0 fusion.377
  1107.6 198.7 %while.79 = (s32[]{:T(128)}, f32[512,8,64]{0,2,1:T(8,128)}, bf16[8,512,1024]{2,1,0:T(8,128)(2,1)}, bf16[8,512,8,64]{1,3,2,0:T(8,128)(2,1)}, s32[512]{0:T(512)S(1...) while((s32[]{:T(128)}, f32[512,8,64]{0,2,1:T(8,128)}, ...), condition=%wide.region_32.33_spmd.clone, body=%wide.region_31.32_spmd.clone.sunk | while | flops 1367353856 | bytes 102045944 | solution.py:270
  1341.5 110.5 %reduce-scatter.9.cloned.1.call-done = bf16[512,1024]{1,0:T(8,128)(2,1)} async-done(((bf16[4096,1024]{1,0:T(8,128)(2,1)}), bf16[512,1024]{1,0:T(8,128)(2,1)}) %reduce-scatter.9.cloned.1.call-update) | async-done | bytes 1048592 | tf_op jit(solution)/shard_map/reduce_scatter | solution.py:275
  1475.0 34.2 %reduce-scatter.15.cloned.1.call-done = bf16[128,2048]{1,0:T(8,128)(2,1)} async-done(((bf16[512,2048]{1,0:T(8,128)(2,1)}), bf16[128,2048]{1,0:T(8,128)(2,1)}) %reduce-scatter.15.cloned.1.call-update) | async-done | bytes 524304 | tf_op jit(solution)/shard_map/reduce_scatter | solution.py:301
  1509.2 34.0 %reduce-scatter.17.cloned.1.call-done = bf16[512,512]{1,0:T(8,128)(2,1)} async-done(((bf16[2048,512]{1,0:T(8,128)(2,1)}), bf16[512,512]{1,0:T(8,128)(2,1)}) %reduce-scatter.17.cloned.1.call-update) | async-done | bytes 524304 | tf_op jit(solution)/shard_map/reduce_scatter | solution.py:304
  1543.2 30.9 %reduce-scatter.11.cloned.1.call-done = bf16[128,1536]{1,0:T(8,128)(2,1)} async-done(((bf16[512,1536]{1,0:T(8,128)(2,1)}), bf16[128,1536]{1,0:T(8,128)(2,1)}) %reduce-scatter.11.cloned.1.call-update) | async-done | bytes 393232 | tf_op jit(solution)/shard_map/reduce_scatter | solution.py:295
  1580.5 10.5 all-reduce.9
  1591.6 21.9 %all-reduce.7 = (bf16[128]{0:T(256)(128)(2,1)S(1)}, bf16[128]{0:T(256)(128)(2,1)S(1)}, bf16[128]{0:T(256)(128)(2,1)S(1)}, bf16[128]{0:T(256)(128)(2,1)S(1)}, bf1...) all-reduce(bf16[128]{0:T(256)(128)(2,1)S(1)} %dynamic-slice.1, ...), channel_id=1, replica_groups=mesh['ctx'=8,'fsdp'=4] {'ctx'}, use_global_device_ids=true, to_apply=%region_47.48 | all-reduce | flops 1280 | bytes 5120 | tf_op jit(solution)/shard_map/psum | solution.py:334
  1617.1 51.0 %all-reduce.12.cloned.1.call-done = (bf16[128,1536]{1,0:T(8,128)(2,1)}, bf16[128,512]{1,0:T(8,128)(2,1)}, bf16[128,2048]{1,0:T(8,128)(2,1)}, bf16[512,512]{1,0:T(8,128)(2,1)}) async-done(((bf16[128,1536]{1,0:T(8,128)(2,1)}, bf16[128,512]{1,0:T(8,128)(2,1)}, bf16[128,2048]{1,0:T(8,128)(2,1)}, bf16[512,512]{1,0:T(8,128)(2,1)}), (bf16[128,1536]{1,0:T(8,128)(2,1)}, bf16[128,512]{1,0:T(8,128)(2,1)}, ...) | async-done | bytes 1572880 | tf_op jit(solution)/shard_map/psum | solution.py:330
  (934 shorter events, 971.8 us)
Async XLA Ops:
  7.2 24.8 %all-gather.13.cloned.1.call-start = ((), (), s32[]{:S(2)}) async-start(), calls=%async_computation.6 | async-start | bytes 1966080 | tf_op jit(solution)/shard_map/all_gather | solution.py:146
  7.9 851.6 %all-gather.15.cloned.1.call-start = ((), (), s32[]{:S(2)}) async-start(), calls=%async_computation.7 | async-start | bytes 2621440 | tf_op jit(solution)/shard_map/all_gather | solution.py:148
  8.7 860.9 %all-gather.17.cloned.1.call-start = ((), (), s32[]{:S(2)}) async-start(), calls=%async_computation.8 | async-start | bytes 2621440 | tf_op jit(solution)/shard_map/all_gather | solution.py:149
  34.9 186.2 %copy-start.97 = (s32[2,1,512]{2,1,0:T(1,128)S(1)}, s32[2,1,512]{2,1,0:T(1,128)}, u32[]{:S(2)}) copy-start(s32[2,1,512]{2,1,0:T(1,128)} %param.29) | copy-start | bytes 12292
  34.9 28.7 %collective-permute-start.7 = (bf16[512,1024]{1,0:T(8,128)(2,1)S(1)}, bf16[512,1024]{1,0:T(8,128)(2,1)S(1)}, u32[]{:S(2)}, u32[]{:S(2)}) collective-permute-start(bf16[512,1024]{1,0:T(8,128)(2,1)S(1)} %slice.88), channel_id=1, source_target_pairs={{0,4},{4,8},{8,12},{12,16},{16,20},{20,24},{24,28},{28,0},{1,5},{5... | collective-permute-start | bytes 3145736 | tf_op jit(solution)/shard_map/ppermute | solution.py:21
  37.7 48.4 %collective-permute-start = (bf16[512,1024]{1,0:T(8,128)(2,1)S(1)}, bf16[512,1024]{1,0:T(8,128)(2,1)S(1)}, u32[]{:S(2)}, u32[]{:S(2)}) collective-permute-start(bf16[512,1024]{1,0:T(8,128)(2,1)S(1)} %slice.84), channel_id=1, source_target_pairs={{0,4},{4,8},{8,12},{12,16},{16,20},{20,24},{24,28},{28,0},{1,5},{5... | collective-permute-start | bytes 3145736 | tf_op jit(solution)/shard_map/ppermute | solution.py:21
  63.6 44.9 %collective-permute-start.8 = (bf16[512,1024]{1,0:T(8,128)(2,1)S(1)}, bf16[512,1024]{1,0:T(8,128)(2,1)S(1)}, u32[]{:S(2)}, u32[]{:S(2)}) collective-permute-start(bf16[512,1024]{1,0:T(8,128)(2,1)S(1)} %collective-permute-done.7), channel_id=1, source_target_pairs={{0,4},{4,8},{8,12},{12,16},{16,20},{20,24},{24,28},{28,0},{1,5},{5... | collective-permute-start | bytes 3145736 | tf_op jit(solution)/shard_map/ppermute | solution.py:21
  86.1 44.9 %collective-permute-start.1 = (bf16[512,1024]{1,0:T(8,128)(2,1)S(1)}, bf16[512,1024]{1,0:T(8,128)(2,1)S(1)}, u32[]{:S(2)}, u32[]{:S(2)}) collective-permute-start(bf16[512,1024]{1,0:T(8,128)(2,1)S(1)} %collective-permute-done), channel_id=1, source_target_pairs={{0,4},{4,8},{8,12},{12,16},{16,20},{20,24},{24,28},{28,0},{1,5},{5... | collective-permute-start | bytes 3145736 | tf_op jit(solution)/shard_map/ppermute | solution.py:21
  108.6 44.9 %collective-permute-start.9 = (bf16[512,1024]{1,0:T(8,128)(2,1)S(1)}, bf16[512,1024]{1,0:T(8,128)(2,1)S(1)}, u32[]{:S(2)}, u32[]{:S(2)}) collective-permute-start(bf16[512,1024]{1,0:T(8,128)(2,1)S(1)} %collective-permute-done.8), channel_id=1, source_target_pairs={{0,4},{4,8},{8,12},{12,16},{16,20},{20,24},{24,28},{28,0},{1,5},{5... | collective-permute-start | bytes 3145736 | tf_op jit(solution)/shard_map/ppermute | solution.py:21
  131.0 181.5 %copy-start.53 = (bf16[512,1024]{1,0:T(8,128)(2,1)}, bf16[512,1024]{1,0:T(8,128)(2,1)S(1)}, u32[]{:S(2)}) copy-start(bf16[512,1024]{1,0:T(8,128)(2,1)S(1)} %collective-permute-done.1) | copy-start | bytes 3145732
  131.0 45.0 %collective-permute-start.2 = (bf16[512,1024]{1,0:T(8,128)(2,1)S(1)}, bf16[512,1024]{1,0:T(8,128)(2,1)}, u32[]{:S(2)}, u32[]{:S(2)}) collective-permute-start(bf16[512,1024]{1,0:T(8,128)(2,1)S(1)} %collective-permute-done.1), channel_id=1, source_target_pairs={{0,4},{4,8},{8,12},{12,16},{16,20},{20,24},{24,28},{28,0},{1,5},{5... | collective-permute-start | bytes 3145736 | tf_op jit(solution)/shard_map/ppermute | solution.py:21
  131.1 1206.3 %reduce-scatter.7.cloned.1.call-start = ((), (), s32[]{:S(2)}) async-start(), calls=%async_computation.9 | async-start | bytes 9437184 | tf_op jit(solution)/shard_map/reduce_scatter | solution.py:275
  153.5 159.0 %copy-start.52 = (bf16[512,1024]{1,0:T(8,128)(2,1)}, bf16[512,1024]{1,0:T(8,128)(2,1)S(1)}, u32[]{:S(2)}) copy-start(bf16[512,1024]{1,0:T(8,128)(2,1)S(1)} %collective-permute-done.9) | copy-start | bytes 3145732
  153.5 45.0 %collective-permute-start.10 = (bf16[512,1024]{1,0:T(8,128)(2,1)S(1)}, bf16[512,1024]{1,0:T(8,128)(2,1)}, u32[]{:S(2)}, u32[]{:S(2)}) collective-permute-start(bf16[512,1024]{1,0:T(8,128)(2,1)S(1)} %collective-permute-done.9), channel_id=1, source_target_pairs={{0,4},{4,8},{8,12},{12,16},{16,20},{20,24},{24,28},{28,0},{1,5},{5... | collective-permute-start | bytes 3145736 | tf_op jit(solution)/shard_map/ppermute | solution.py:21
  176.1 44.9 %collective-permute-start.3 = (bf16[512,1024]{1,0:T(8,128)(2,1)}, bf16[512,1024]{1,0:T(8,128)(2,1)}, u32[]{:S(2)}, u32[]{:S(2)}) collective-permute-start(bf16[512,1024]{1,0:T(8,128)(2,1)} %collective-permute-done.2), channel_id=1, source_target_pairs={{0,4},{4,8},{8,12},{12,16},{16,20},{20,24},{24,28},{28,0},{1,5},{5... | collective-permute-start | bytes 3145736 | tf_op jit(solution)/shard_map/ppermute | solution.py:21
  198.6 196.7 %collective-permute-start.11 = (bf16[512,1024]{1,0:T(8,128)(2,1)}, bf16[512,1024]{1,0:T(8,128)(2,1)}, u32[]{:S(2)}, u32[]{:S(2)}) collective-permute-start(bf16[512,1024]{1,0:T(8,128)(2,1)} %collective-permute-done.10), channel_id=1, source_target_pairs={{0,4},{4,8},{8,12},{12,16},{16,20},{20,24},{24,28},{28,0},{1,5},{5... | collective-permute-start | bytes 3145736 | tf_op jit(solution)/shard_map/ppermute | solution.py:21
  221.0 174.3 %collective-permute-start.4 = (bf16[512,1024]{1,0:T(8,128)(2,1)}, bf16[512,1024]{1,0:T(8,128)(2,1)}, u32[]{:S(2)}, u32[]{:S(2)}) collective-permute-start(bf16[512,1024]{1,0:T(8,128)(2,1)} %collective-permute-done.3), channel_id=1, source_target_pairs={{0,4},{4,8},{8,12},{12,16},{16,20},{20,24},{24,28},{28,0},{1,5},{5... | collective-permute-start | bytes 3145736 | tf_op jit(solution)/shard_map/ppermute | solution.py:21
  380.7 482.0 %copy-start.65 = (f32[4,1,128]{2,1,0:T(1,128)}, f32[4,1,128]{2,1,0:T(1,128)S(1)}, u32[]{:S(2)}) copy-start(f32[4,1,128]{2,1,0:T(1,128)S(1)} %convert_element_type.308) | copy-start | bytes 6148
  385.8 509.1 %copy-start.58 = (f32[4,1,128]{2,1,0:T(1,128)}, f32[4,1,128]{2,1,0:T(1,128)S(1)}, u32[]{:S(2)}) copy-start(f32[4,1,128]{2,1,0:T(1,128)S(1)} %convert_element_type.307) | copy-start | bytes 6148
  395.3 461.5 %copy-start.17 = (bf16[512,512]{1,0:T(8,128)(2,1)}, bf16[512,512]{1,0:T(8,128)(2,1)S(1)}, u32[]{:S(2)}) copy-start(bf16[512,512]{1,0:T(8,128)(2,1)S(1)} %all_gather.43) | copy-start | bytes 1572868
  395.3 32.8 %collective-permute-start.12 = (bf16[512,1024]{1,0:T(8,128)(2,1)}, bf16[512,1024]{1,0:T(8,128)(2,1)}, u32[]{:S(2)}, u32[]{:S(2)}) collective-permute-start(bf16[512,1024]{1,0:T(8,128)(2,1)} %collective-permute-done.11), channel_id=1, source_target_pairs={{0,4},{4,8},{8,12},{12,16},{16,20},{20,24},{24,28},{28,0},{1,5},{5... | collective-permute-start | bytes 3145736 | tf_op jit(solution)/shard_map/ppermute | solution.py:21
  395.3 51.5 %collective-permute-start.5 = (bf16[512,1024]{1,0:T(8,128)(2,1)}, bf16[512,1024]{1,0:T(8,128)(2,1)}, u32[]{:S(2)}, u32[]{:S(2)}) collective-permute-start(bf16[512,1024]{1,0:T(8,128)(2,1)} %collective-permute-done.4), channel_id=1, source_target_pairs={{0,4},{4,8},{8,12},{12,16},{16,20},{20,24},{24,28},{28,0},{1,5},{5... | collective-permute-start | bytes 3145736 | tf_op jit(solution)/shard_map/ppermute | solution.py:21
  428.1 44.0 %collective-permute-start.13 = (bf16[512,1024]{1,0:T(8,128)(2,1)}, bf16[512,1024]{1,0:T(8,128)(2,1)}, u32[]{:S(2)}, u32[]{:S(2)}) collective-permute-start(bf16[512,1024]{1,0:T(8,128)(2,1)} %collective-permute-done.12), channel_id=1, source_target_pairs={{0,4},{4,8},{8,12},{12,16},{16,20},{20,24},{24,28},{28,0},{1,5},{5... | collective-permute-start | bytes 3145736 | tf_op jit(solution)/shard_map/ppermute | solution.py:21
  446.8 44.4 %collective-permute-start.6 = (bf16[512,1024]{1,0:T(8,128)(2,1)}, bf16[512,1024]{1,0:T(8,128)(2,1)}, u32[]{:S(2)}, u32[]{:S(2)}) collective-permute-start(bf16[512,1024]{1,0:T(8,128)(2,1)} %collective-permute-done.5), channel_id=1, source_target_pairs={{0,4},{4,8},{8,12},{12,16},{16,20},{20,24},{24,28},{28,0},{1,5},{5... | collective-permute-start | bytes 3145736 | tf_op jit(solution)/shard_map/ppermute | solution.py:21
  1099.1 352.9 %reduce-scatter.9.cloned.1.call-start = ((), (), s32[]{:S(2)}) async-start(), calls=%async_computation.10 | async-start | bytes 9437184 | tf_op jit(solution)/shard_map/reduce_scatter | solution.py:275
  1306.4 168.6 %reduce-scatter.13.cloned.1.call-start = ((), (), s32[]{:S(2)}) async-start(), calls=%async_computation.12 | async-start | bytes 655360 | tf_op jit(solution)/shard_map/reduce_scatter | solution.py:298
  1309.3 199.9 %reduce-scatter.15.cloned.1.call-start = ((), (), s32[]{:S(2)}) async-start(), calls=%async_computation.13 | async-start | bytes 2621440 | tf_op jit(solution)/shard_map/reduce_scatter | solution.py:301
  1315.9 227.3 %reduce-scatter.17.cloned.1.call-start = ((), (), s32[]{:S(2)}) async-start(), calls=%async_computation.14 | async-start | bytes 2621440 | tf_op jit(solution)/shard_map/reduce_scatter | solution.py:304
  1322.0 252.1 %reduce-scatter.11.cloned.1.call-start = ((), (), s32[]{:S(2)}) async-start(), calls=%async_computation.11 | async-start | bytes 1966080 | tf_op jit(solution)/shard_map/reduce_scatter | solution.py:295
  1337.3 114.7 %copy-start.72 = (f32[512]{0:T(512)S(1)}, f32[512]{0:T(512)}, u32[]{:S(2)}) copy-start(f32[512]{0:T(512)} %copy-done.71) | copy-start | bytes 6148
  1337.3 114.7 %copy-start.80 = (f32[512]{0:T(512)S(1)}, f32[512]{0:T(512)}, u32[]{:S(2)}) copy-start(f32[512]{0:T(512)} %copy-done.79) | copy-start | bytes 6148
  1456.5 211.5 %all-reduce.12.cloned.1.call-start = ((), (), s32[]{:S(2)}) async-start(), calls=%async_computation.15 | async-start | bytes 3145728 | tf_op jit(solution)/shard_map/psum | solution.py:330
  (133 other events, 1935.1 us)
Sparse Core Ops, SparseCore 0:
  9.6 22.3 all-gather.12
  33.5 22.5 all-gather.14
  131.2 23.0 all-gather.16
  1099.3 145.2 reduce-scatter.6
  1306.5 145.5 reduce-scatter.8
  1454.4 20.6 reduce-scatter.12
  1477.7 31.4 reduce-scatter.14
  1511.7 31.4 reduce-scatter.16
  1545.9 28.1 reduce-scatter.10
  1577.8 90.2 all-reduce.11
